TPU v7x, 32 devices: a whole 2x2x4 slice. The times are simulated.
32 devices in a mesh: groups: 2 (over x), spatial: 16 (over z, y, core).
Axes of the slice: x: 2, y: 2, z: 4, core: 2. Of those that a mesh axis runs over, the one named last changes fastest.
Arguments:
- fields: bfloat16 [1024, 128, 768], P(('groups', 'spatial')), parts along dimension 0, may hold values from -6 to 6
- norm1_gain: float32 [768], replicated, may hold values from 0.5 to 1.5
- norm1_bias: float32 [768], replicated, may hold values from -3 to 3
- spectral_w1: float32 [2, 8, 96, 96], replicated, may hold values from -0.4375 to 0.4375
- spectral_b1: float32 [2, 8, 96], replicated, may hold values from -3 to 3
- spectral_w2: float32 [2, 8, 96, 96], replicated, may hold values from -0.4375 to 0.4375
- spectral_b2: float32 [2, 8, 96], replicated, may hold values from -3 to 3
- norm2_gain: float32 [768], replicated, may hold values from 0.5 to 1.5
- norm2_bias: float32 [768], replicated, may hold values from -3 to 3
- fc1_weight: bfloat16 [768, 3072], replicated, may hold values from -0.21875 to 0.21875
- fc1_bias: float32 [3072], replicated, may hold values from -3 to 3
- fc2_weight: bfloat16 [3072, 768], replicated, may hold values from -0.109375 to 0.109375
- fc2_bias: float32 [768], replicated, may hold values from -3 to 3
Outputs:
- next_state: bfloat16 [1024, 128, 768], P(('groups', 'spatial')), parts along dimension 0
- anomaly: bfloat16 [1024, 128, 768], P(('groups', 'spatial')), parts along dimension 0
There are 2 independent parts, one for each index of `groups`. A program takes and returns all parts, laid end to end along the dimension named above; an argument that names none is the same for every part. Nothing has to cross between parts.
All inputs are finite; a program needn't handle non-finite values.
Results may differ from a plain program's by a relative error of at most 0.0056.
Values may be sent and summed in bfloat16 or wider, within the bound.
A program may use at most 192 MiB of HBM per device.

v0:
```python
import math
import jax
import jax.numpy as jnp
from jax import lax
from jax.sharding import PartitionSpec as P

MEMBERS = 8
EPSILON = 1e-06
SHRINK = 0.01
FULL_PRECISION = lax.Precision.HIGHEST


def from_behind(block, axis, distance):
    devices = range(lax.axis_size(axis))
    route = [((i - distance) % len(devices), i) for i in devices]
    return lax.ppermute(block, axis, route)


def layer_norm(values, gain, offset_term):
    center = values - jnp.mean(values, axis=-1, keepdims=True)
    spread = jnp.mean(center * center, axis=-1, keepdims=True)
    return center * lax.rsqrt(spread + EPSILON) * gain + offset_term


def soft_shrink(values):
    return jnp.where(
        values > SHRINK, values - SHRINK, jnp.where(values < -SHRINK, values + SHRINK, 0.0)
    )


def contract(form, left, right):
    return jnp.einsum(form, left, right, precision=FULL_PRECISION)


def block_product(values, weight):
    return jnp.einsum("...bi,bio->...bo", values, weight, precision=FULL_PRECISION)


def angle_table(first_len, second_len, modulus):
    first_index = lax.broadcasted_iota(jnp.int32, (first_len, second_len), 0)
    second_index = lax.broadcasted_iota(jnp.int32, (first_len, second_len), 1)
    phase = first_index * second_index % modulus
    return phase.astype(jnp.float32) * (2.0 * math.pi / modulus)


def spectral_layer(real_part, imag_part, w_first, b_first, w_second, b_second):
    shape = real_part.shape
    block_count = w_first.shape[1]
    split_shape = shape[:-1] + (block_count, shape[-1] // block_count)
    real_part = real_part.reshape(split_shape)
    imag_part = imag_part.reshape(split_shape)
    hidden_real = jax.nn.relu(
        block_product(real_part, w_first[0]) - block_product(imag_part, w_first[1]) + b_first[0]
    )
    hidden_imag = jax.nn.relu(
        block_product(imag_part, w_first[0]) + block_product(real_part, w_first[1]) + b_first[1]
    )
    mixed_real = (
        block_product(hidden_real, w_second[0])
        - block_product(hidden_imag, w_second[1])
        + b_second[0]
    )
    mixed_imag = (
        block_product(hidden_imag, w_second[0])
        + block_product(hidden_real, w_second[1])
        + b_second[1]
    )
    return (soft_shrink(mixed_real).reshape(shape), soft_shrink(mixed_imag).reshape(shape))


def longitude_forward(normed, lon_len):
    angles = angle_table(lon_len, lon_len // 2, lon_len)
    factor = 1.0 / math.sqrt(lon_len)
    real_part = contract("rld,lk->rkd", normed, jnp.cos(angles) * factor)
    imag_part = -contract("rld,lk->rkd", normed, jnp.sin(angles) * factor)
    return (real_part, imag_part)


def longitude_inverse(real_part, imag_part, lon_len):
    half_len = lon_len // 2
    angles = angle_table(lon_len, half_len, lon_len)
    column_index = lax.broadcasted_iota(jnp.int32, (1, half_len), 1)
    weights = jnp.where(column_index == 0, 1.0, 2.0) / math.sqrt(lon_len)
    cosine_table = jnp.cos(angles) * weights
    sine_table = jnp.sin(angles) * weights
    return contract("rkd,lk->rld", real_part, cosine_table) - contract(
        "rkd,lk->rld", imag_part, sine_table
    )


def latitude_work(real_part, imag_part, w_first, b_first, w_second, b_second):
    member_rows, mode_count, channels = real_part.shape
    lat_len = member_rows // MEMBERS
    angles = angle_table(lat_len, lat_len, lat_len)
    factor = 1.0 / math.sqrt(lat_len)
    cosine_table = jnp.cos(angles) * factor
    sine_table = jnp.sin(angles) * factor
    grid_real = real_part.reshape(MEMBERS, lat_len, mode_count, channels)
    grid_imag = imag_part.reshape(MEMBERS, lat_len, mode_count, channels)
    spec_real = contract("qp,mpkd->mqkd", cosine_table, grid_real) + contract(
        "qp,mpkd->mqkd", sine_table, grid_imag
    )
    spec_imag = contract("qp,mpkd->mqkd", cosine_table, grid_imag) - contract(
        "qp,mpkd->mqkd", sine_table, grid_real
    )
    mixed_real, mixed_imag = spectral_layer(
        spec_real, spec_imag, w_first, b_first, w_second, b_second
    )
    back_real = contract("qp,mpkd->mqkd", cosine_table, mixed_real) - contract(
        "qp,mpkd->mqkd", sine_table, mixed_imag
    )
    back_imag = contract("qp,mpkd->mqkd", cosine_table, mixed_imag) + contract(
        "qp,mpkd->mqkd", sine_table, mixed_real
    )
    return (
        back_real.reshape(member_rows, mode_count, channels),
        back_imag.reshape(member_rows, mode_count, channels),
    )


def on_device(
    fields,
    norm1_gain,
    norm1_bias,
    spectral_w1,
    spectral_b1,
    spectral_w2,
    spectral_b2,
    norm2_gain,
    norm2_bias,
    fc1_weight,
    fc1_bias,
    fc2_weight,
    fc2_bias,
):
    row_count, lon_len, channels = fields.shape
    state = fields.astype(jnp.float32)
    normed = layer_norm(state, norm1_gain, norm1_bias)
    real_part, imag_part = longitude_forward(normed, lon_len)
    real_part, imag_part = (
        lax.all_to_all(real_part, "spatial", split_axis=1, concat_axis=0, tiled=True),
        lax.all_to_all(imag_part, "spatial", split_axis=1, concat_axis=0, tiled=True),
    )
    real_part, imag_part = latitude_work(
        real_part, imag_part, spectral_w1, spectral_b1, spectral_w2, spectral_b2
    )
    real_part, imag_part = (
        lax.all_to_all(real_part, "spatial", split_axis=0, concat_axis=1, tiled=True),
        lax.all_to_all(imag_part, "spatial", split_axis=0, concat_axis=1, tiled=True),
    )
    filtered = longitude_inverse(real_part, imag_part, lon_len)
    residual = (filtered + normed + state).reshape(row_count * lon_len, channels)
    normed2 = layer_norm(residual, norm2_gain, norm2_bias).astype(jnp.bfloat16)
    hidden = jax.nn.gelu(
        jnp.dot(normed2, fc1_weight, preferred_element_type=jnp.float32) + fc1_bias,
        approximate=False,
    ).astype(jnp.bfloat16)
    updated = residual + jnp.dot(hidden, fc2_weight, preferred_element_type=jnp.float32) + fc2_bias
    next_state = updated.astype(jnp.bfloat16).reshape(row_count, lon_len, channels)
    device_count = lax.axis_size("spatial")
    member_span = device_count // MEMBERS
    state_values = next_state.astype(jnp.float32)

    def advance(counter, state_pair):
        moving, summed = state_pair
        moving = from_behind(moving, "spatial", member_span)
        return (moving, summed + moving.astype(jnp.float32))

    ignored, summed = lax.fori_loop(0, MEMBERS - 1, advance, (next_state, state_values))
    ensemble_mean = summed / MEMBERS
    anomaly = (state_values - ensemble_mean).astype(jnp.bfloat16)
    return (next_state, anomaly)


def solution(mesh):
    placed = (
        P(("groups", "spatial"), None, None),
        P(),
        P(),
        P(),
        P(),
        P(),
        P(),
        P(),
        P(),
        P(),
        P(),
        P(),
        P(),
    )
    return jax.shard_map(
        on_device,
        mesh=mesh,
        in_specs=placed,
        out_specs=(P(("groups", "spatial"), None, None), P(("groups", "spatial"), None, None)),
        check_vma=False,
    )
```

profile of v0, /device:TPU:0, one launch (start us, length us, event | category | flops | bytes accessed | tf_op | source)
XLA Modules:
  0.0 2131.6 jit_solution(12978921306262983575)
XLA Ops:
  7.6 9.6 negate_bitcast_fusion
  17.2 6.6 copy.58
  23.8 7.5 all-to-all-start.1
  31.3 12.0 fusion.94
  43.3 6.3 copy.55
  49.6 95.7 %all-to-all-done.1 = f32[32,64,768]{2,0,1:T(8,128)} async-done(((f32[32,64,768]{2,0,1:T(8,128)}), f32[32,64,768]{2,0,1:T(8,128)}, u32[]{:S(2)}, u32[]{:S(2)}) %all-to-all-start.1) | async-done | bytes 6291488 | tf_op jit(solution)/shard_map/all_to_all | solution.py:142
  145.3 28.5 %all-to-all-start = ((f32[32,64,768]{2,0,1:T(8,128)}), f32[32,64,768]{2,0,1:T(8,128)}, u32[]{:S(2)}, u32[]{:S(2)}) async-start(f32[32,64,768]{2,0,1:T(8,128)} %copy.55), calls=%async_computation | async-start | bytes 12582912 | tf_op jit(solution)/shard_map/all_to_all | solution.py:141
  177.4 7.9 fusion.74
  185.3 7.8 fusion.76
  193.1 94.8 %all-to-all-done = f32[32,64,768]{2,0,1:T(8,128)} async-done(((f32[32,64,768]{2,0,1:T(8,128)}), f32[32,64,768]{2,0,1:T(8,128)}, u32[]{:S(2)}, u32[]{:S(2)}) %all-to-all-start) | async-done | bytes 6291488 | tf_op jit(solution)/shard_map/all_to_all | solution.py:141
  294.3 7.9 subtract_bitcast_fusion.1
  302.2 9.9 reshape.102
  312.1 13.7 fusion.58
  325.9 9.9 fusion.60
  335.7 8.2 add_bitcast_fusion.1
  343.9 9.9 reshape.101
  353.8 13.1 add_maximum_fusion
  367.0 9.5 fusion.50
  376.4 9.8 fusion.52
  386.3 9.6 add_maximum_fusion.1
  395.9 14.9 select_bitcast_fusion
  410.8 11.0 copy.68
  421.8 9.6 reshape.104
  431.4 12.2 select_bitcast_fusion.1
  443.7 11.0 copy.67
  454.7 9.6 reshape.103
  464.2 8.3 fusion.128
  472.5 8.7 subtract_bitcast_fusion
  481.8 6.6 copy.70
  488.4 28.3 %all-to-all-start.2 = ((f32[512,4,768]{2,1,0:T(4,128)}), f32[512,4,768]{2,1,0:T(4,128)}, u32[]{:S(2)}, u32[]{:S(2)}) async-start(f32[512,4,768]{2,1,0:T(4,128)} %copy.70), calls=%async_computation.2 | async-start | bytes 12582912 | tf_op jit(solution)/shard_map/all_to_all | solution.py:148
  516.7 8.6 fusion.126
  525.3 6.7 add_bitcast_fusion
  532.5 6.7 copy.74
  539.2 91.5 %all-to-all-done.2 = f32[512,4,768]{2,1,0:T(4,128)} async-done(((f32[512,4,768]{2,1,0:T(4,128)}), f32[512,4,768]{2,1,0:T(4,128)}, u32[]{:S(2)}, u32[]{:S(2)}) %all-to-all-start.2) | async-done | bytes 6291488 | tf_op jit(solution)/shard_map/all_to_all | solution.py:148
  630.7 28.5 %all-to-all-start.3 = ((f32[512,4,768]{2,1,0:T(4,128)}), f32[512,4,768]{2,1,0:T(4,128)}, u32[]{:S(2)}, u32[]{:S(2)}) async-start(f32[512,4,768]{2,1,0:T(4,128)} %copy.74), calls=%async_computation.3 | async-start | bytes 12582912 | tf_op jit(solution)/shard_map/all_to_all | solution.py:149
  663.3 6.7 copy.72
  670.0 7.7 all_to_all.57
  677.7 95.6 %all-to-all-done.3 = f32[512,4,768]{2,1,0:T(4,128)} async-done(((f32[512,4,768]{2,1,0:T(4,128)}), f32[512,4,768]{2,1,0:T(4,128)}, u32[]{:S(2)}, u32[]{:S(2)}) %all-to-all-start.3) | async-done | bytes 6291488 | tf_op jit(solution)/shard_map/all_to_all | solution.py:149
  777.3 6.7 copy.76
  784.1 7.9 all_to_all.61
  792.0 15.1 fusion.134
  807.1 19.1 fusion.262
  830.9 126.4 %fusion.2.clone.6 = bf16[4096,3072]{1,0:T(8,128)(2,1)} fusion(bf16[4096,768]{1,0:T(8,128)(2,1)S(1)} %fusion.47, bf16[768,3072]{1,0:T(8,128)(2,1)} %param.24, f32[3072]{0:T(1024)S(1)} %copy-done.22), kind=kOutput, calls=%fused_computation.4.clone.clone.clone.clone.clone.1 | convolution fusion | flops 20157825024 | bytes 36188160 | tf_op jit(solution)/shard_map/dot_general | solution.py:155
  957.2 26.3 %fusion.49 = bf16[4096,768]{1,0:T(8,128)(2,1)S(1)} fusion(f32[32,128,768]{2,1,0:T(8,128)} %copy-done, bf16[3072,768]{1,0:T(8,128)(2,1)} %param.26, f32[768]{0:T(1024)S(1)} %copy-done.23, bf16[4096,3072]{1,0:T(8,128)(2,1)} %fusion.2.clone.6), kind=kOutput, calls=%fused_computation.62 | convolution fusion | flops 19336790016 | bytes 48761856 | tf_op jit(solution)/shard_map/dot_general | solution.py:158
  992.4 1127.6 %while.12 = (s32[]{:T(128)}, bf16[32,128,768]{2,1,0:T(8,128)(2,1)}, f32[32,128,768]{2,1,0:T(8,128)}, s32[]{:T(128)}) while((s32[]{:T(128)}, bf16[32,128,768]{2,1,0:T(8,128)(2,1)}, f32[32,128,768]{2,1,0:T(8,128)}, s32[]{:T(128)}) %tuple.26), condition=%wide.region_5.6_spmd, body=%wide.region_4.5_spmd.sunk | while | flops 6291458 | bytes 69206104 | solution.py:169
  992.6 9.1 collective-permute-start
  1001.7 154.1 %collective-permute-done = bf16[32,128,768]{2,1,0:T(8,128)(2,1)} collective-permute-done((bf16[32,128,768]{2,1,0:T(8,128)(2,1)}, bf16[32,128,768]{2,1,0:T(8,128)(2,1)}, u32[]{:S(2)}, u32[]{:S(2)}) %collective-permute-start) | collective-permute-done | bytes 6291488 | tf_op jit(solution)/shard_map/while/body/eval_jaxpr/ppermute | solution.py:16
  1155.7 6.1 copy.114
  1161.9 13.2 convert_add_fusion.3
  1175.1 140.2 %collective-permute-done = bf16[32,128,768]{2,1,0:T(8,128)(2,1)} collective-permute-done((bf16[32,128,768]{2,1,0:T(8,128)(2,1)}, bf16[32,128,768]{2,1,0:T(8,128)(2,1)}, u32[]{:S(2)}, u32[]{:S(2)}) %collective-permute-start) | collective-permute-done | bytes 6291488 | tf_op jit(solution)/shard_map/while/body/eval_jaxpr/ppermute | solution.py:16
  1315.3 6.1 copy.114
  1321.5 13.2 convert_add_fusion.3
  1334.7 139.4 %collective-permute-done = bf16[32,128,768]{2,1,0:T(8,128)(2,1)} collective-permute-done((bf16[32,128,768]{2,1,0:T(8,128)(2,1)}, bf16[32,128,768]{2,1,0:T(8,128)(2,1)}, u32[]{:S(2)}, u32[]{:S(2)}) %collective-permute-start) | collective-permute-done | bytes 6291488 | tf_op jit(solution)/shard_map/while/body/eval_jaxpr/ppermute | solution.py:16
  1474.1 6.1 copy.114
  1480.3 13.2 convert_add_fusion.3
  1493.5 138.5 %collective-permute-done = bf16[32,128,768]{2,1,0:T(8,128)(2,1)} collective-permute-done((bf16[32,128,768]{2,1,0:T(8,128)(2,1)}, bf16[32,128,768]{2,1,0:T(8,128)(2,1)}, u32[]{:S(2)}, u32[]{:S(2)}) %collective-permute-start) | collective-permute-done | bytes 6291488 | tf_op jit(solution)/shard_map/while/body/eval_jaxpr/ppermute | solution.py:16
  1638.2 13.2 convert_add_fusion.3
  1651.4 137.7 %collective-permute-done = bf16[32,128,768]{2,1,0:T(8,128)(2,1)} collective-permute-done((bf16[32,128,768]{2,1,0:T(8,128)(2,1)}, bf16[32,128,768]{2,1,0:T(8,128)(2,1)}, u32[]{:S(2)}, u32[]{:S(2)}) %collective-permute-start) | collective-permute-done | bytes 6291488 | tf_op jit(solution)/shard_map/while/body/eval_jaxpr/ppermute | solution.py:16
  1795.2 13.2 convert_add_fusion.3
  1808.4 136.8 %collective-permute-done = bf16[32,128,768]{2,1,0:T(8,128)(2,1)} collective-permute-done((bf16[32,128,768]{2,1,0:T(8,128)(2,1)}, bf16[32,128,768]{2,1,0:T(8,128)(2,1)}, u32[]{:S(2)}, u32[]{:S(2)}) %collective-permute-start) | collective-permute-done | bytes 6291488 | tf_op jit(solution)/shard_map/while/body/eval_jaxpr/ppermute | solution.py:16
  1951.4 13.2 convert_add_fusion.3
  1964.6 136.0 %collective-permute-done = bf16[32,128,768]{2,1,0:T(8,128)(2,1)} collective-permute-done((bf16[32,128,768]{2,1,0:T(8,128)(2,1)}, bf16[32,128,768]{2,1,0:T(8,128)(2,1)}, u32[]{:S(2)}, u32[]{:S(2)}) %collective-permute-start) | collective-permute-done | bytes 6291488 | tf_op jit(solution)/shard_map/while/body/eval_jaxpr/ppermute | solution.py:16
  2106.7 13.2 convert_add_fusion.3
  2120.0 11.2 subtract_convert_fusion
  (107 shorter events, 63.9 us)
Async XLA Ops:
  0.6 4.6 copy-start.3
  0.6 7.0 copy-start.16
  0.7 7.0 copy-start.18
  5.2 26.0 %copy-start.10 = (f32[32,128]{1,0:T(8,128)}, f32[32,128]{1,0:T(8,128)S(1)}, u32[]{:S(2)}) copy-start(f32[32,128]{1,0:T(8,128)S(1)} %broadcast_multiply_fusion.1) | copy-start | bytes 49156
  7.6 23.6 %copy-start.12 = (f32[32,128]{1,0:T(8,128)}, f32[32,128]{1,0:T(8,128)S(1)}, u32[]{:S(2)}) copy-start(f32[32,128]{1,0:T(8,128)S(1)} %add_rsqrt_fusion) | copy-start | bytes 49156
  23.8 121.5 %all-to-all-start.1 = ((f32[32,64,768]{2,0,1:T(8,128)}), f32[32,64,768]{2,0,1:T(8,128)}, u32[]{:S(2)}, u32[]{:S(2)}) async-start(f32[32,64,768]{2,0,1:T(8,128)} %copy.58), calls=%async_computation.1 | async-start | bytes 12582912 | tf_op jit(solution)/shard_map/all_to_all | solution.py:142
  49.6 124.2 %copy-start.14 = (f32[2,8,96]{2,1,0:T(8,128)S(1)}, f32[2,8,96]{2,1,0:T(8,128)}, u32[]{:S(2)}) copy-start(f32[2,8,96]{2,1,0:T(8,128)} %param.19) | copy-start | bytes 18436
  49.6 124.3 %copy-start.15 = (f32[2,8,96]{2,1,0:T(8,128)S(1)}, f32[2,8,96]{2,1,0:T(8,128)}, u32[]{:S(2)}) copy-start(f32[2,8,96]{2,1,0:T(8,128)} %param.21) | copy-start | bytes 18436
  145.3 142.6 %all-to-all-start = ((f32[32,64,768]{2,0,1:T(8,128)}), f32[32,64,768]{2,0,1:T(8,128)}, u32[]{:S(2)}, u32[]{:S(2)}) async-start(f32[32,64,768]{2,0,1:T(8,128)} %copy.55), calls=%async_computation | async-start | bytes 12582912 | tf_op jit(solution)/shard_map/all_to_all | solution.py:141
  193.1 101.2 %slice-start.10 = ((s8[6291456]{0:T(1024)(128)(4,1)}), s8[2097152]{0:T(1024)(128)(4,1)S(1)}, s32[]{:S(2)}) async-start(s8[6291456]{0:T(1024)(128)(4,1)} %bitcast.204), calls=%async_computation.14 | async-start | bytes 4194304
  287.9 6.4 slice-start.11
  291.6 2.7 copy-start.5
  302.2 9.9 copy-start.6
  312.1 13.7 copy-start.1
  312.1 23.6 %slice-start.4 = ((s8[6291456]{0:T(1024)(128)(4,1)}), s8[4194304]{0:T(1024)(128)(4,1)S(1)}, s32[]{:S(2)}) async-start(s8[6291456]{0:T(1024)(128)(4,1)} %bitcast.193), calls=%async_computation.8 | async-start | bytes 8388608
  312.1 23.6 %slice-start.8 = ((s8[6291456]{0:T(1024)(128)(4,1)}), s8[4194304]{0:T(1024)(128)(4,1)S(1)}, s32[]{:S(2)}) async-start(s8[6291456]{0:T(1024)(128)(4,1)} %bitcast.202), calls=%async_computation.12 | async-start | bytes 8388608
  325.8 9.9 slice-start.5
  325.9 9.9 slice-start.9
  353.8 13.2 copy-start.7
  366.9 9.5 copy-start.8
  366.9 19.3 slice-start
  367.0 19.3 slice-start.6
  376.4 9.9 slice-start.1
  376.4 9.9 slice-start.7
  395.9 14.9 copy-start.2
  421.8 9.6 copy-start.9
  488.4 36.9 %slice-start.2 = ((s8[6291456]{0:T(1024)(128)(4,1)}), s8[2097152]{0:T(1024)(128)(4,1)S(1)}, s32[]{:S(2)}) async-start(s8[6291456]{0:T(1024)(128)(4,1)} %bitcast.184), calls=%async_computation.6 | async-start | bytes 4194304
  488.4 142.3 %all-to-all-start.2 = ((f32[512,4,768]{2,1,0:T(4,128)}), f32[512,4,768]{2,1,0:T(4,128)}, u32[]{:S(2)}, u32[]{:S(2)}) async-start(f32[512,4,768]{2,1,0:T(4,128)} %copy.70), calls=%async_computation.2 | async-start | bytes 12582912 | tf_op jit(solution)/shard_map/all_to_all | solution.py:148
  516.7 8.6 slice-start.3
  630.7 142.6 %all-to-all-start.3 = ((f32[512,4,768]{2,1,0:T(4,128)}), f32[512,4,768]{2,1,0:T(4,128)}, u32[]{:S(2)}, u32[]{:S(2)}) async-start(f32[512,4,768]{2,1,0:T(4,128)} %copy.74), calls=%async_computation.3 | async-start | bytes 12582912 | tf_op jit(solution)/shard_map/all_to_all | solution.py:149
  792.0 15.2 copy-start.11
  792.0 15.2 copy-start.13
  792.0 15.2 copy-start.17
  792.0 15.2 copy-start.19
  826.3 4.6 copy-start
  826.3 1.5 copy-start.20
  826.3 1.5 copy-start.21
  827.8 3.1 copy-start.22
  830.9 126.4 %copy-start.23 = (f32[768]{0:T(1024)S(1)}, f32[768]{0:T(1024)}, u32[]{:S(2)}) copy-start(f32[768]{0:T(1024)} %param.27) | copy-start | bytes 9220
  983.5 8.9 copy-start.4
  992.6 163.1 %collective-permute-start = (bf16[32,128,768]{2,1,0:T(8,128)(2,1)}, bf16[32,128,768]{2,1,0:T(8,128)(2,1)}, u32[]{:S(2)}, u32[]{:S(2)}) collective-permute-start(bf16[32,128,768]{2,1,0:T(8,128)(2,1)} %get-tuple-element.58), channel_id=1, source_target_pairs={{14,0},{15,1},{0,2},{1,3},{2,4},{3,5},{4,6},{5,7},{6,8},{7,9},{8,1... | collective-permute-start | bytes 18874376 | tf_op jit(solution)/shard_map/while/body/eval_jaxpr/ppermute | solution.py:16
  1175.1 140.2 %collective-permute-start = (bf16[32,128,768]{2,1,0:T(8,128)(2,1)}, bf16[32,128,768]{2,1,0:T(8,128)(2,1)}, u32[]{:S(2)}, u32[]{:S(2)}) collective-permute-start(bf16[32,128,768]{2,1,0:T(8,128)(2,1)} %get-tuple-element.58), channel_id=1, source_target_pairs={{14,0},{15,1},{0,2},{1,3},{2,4},{3,5},{4,6},{5,7},{6,8},{7,9},{8,1... | collective-permute-start | bytes 18874376 | tf_op jit(solution)/shard_map/while/body/eval_jaxpr/ppermute | solution.py:16
  1334.7 139.4 %collective-permute-start = (bf16[32,128,768]{2,1,0:T(8,128)(2,1)}, bf16[32,128,768]{2,1,0:T(8,128)(2,1)}, u32[]{:S(2)}, u32[]{:S(2)}) collective-permute-start(bf16[32,128,768]{2,1,0:T(8,128)(2,1)} %get-tuple-element.58), channel_id=1, source_target_pairs={{14,0},{15,1},{0,2},{1,3},{2,4},{3,5},{4,6},{5,7},{6,8},{7,9},{8,1... | collective-permute-start | bytes 18874376 | tf_op jit(solution)/shard_map/while/body/eval_jaxpr/ppermute | solution.py:16
  1493.5 138.5 %collective-permute-start = (bf16[32,128,768]{2,1,0:T(8,128)(2,1)}, bf16[32,128,768]{2,1,0:T(8,128)(2,1)}, u32[]{:S(2)}, u32[]{:S(2)}) collective-permute-start(bf16[32,128,768]{2,1,0:T(8,128)(2,1)} %get-tuple-element.58), channel_id=1, source_target_pairs={{14,0},{15,1},{0,2},{1,3},{2,4},{3,5},{4,6},{5,7},{6,8},{7,9},{8,1... | collective-permute-start | bytes 18874376 | tf_op jit(solution)/shard_map/while/body/eval_jaxpr/ppermute | solution.py:16
  1651.4 137.7 %collective-permute-start = (bf16[32,128,768]{2,1,0:T(8,128)(2,1)}, bf16[32,128,768]{2,1,0:T(8,128)(2,1)}, u32[]{:S(2)}, u32[]{:S(2)}) collective-permute-start(bf16[32,128,768]{2,1,0:T(8,128)(2,1)} %get-tuple-element.58), channel_id=1, source_target_pairs={{14,0},{15,1},{0,2},{1,3},{2,4},{3,5},{4,6},{5,7},{6,8},{7,9},{8,1... | collective-permute-start | bytes 18874376 | tf_op jit(solution)/shard_map/while/body/eval_jaxpr/ppermute | solution.py:16
  1808.4 136.8 %collective-permute-start = (bf16[32,128,768]{2,1,0:T(8,128)(2,1)}, bf16[32,128,768]{2,1,0:T(8,128)(2,1)}, u32[]{:S(2)}, u32[]{:S(2)}) collective-permute-start(bf16[32,128,768]{2,1,0:T(8,128)(2,1)} %get-tuple-element.58), channel_id=1, source_target_pairs={{14,0},{15,1},{0,2},{1,3},{2,4},{3,5},{4,6},{5,7},{6,8},{7,9},{8,1... | collective-permute-start | bytes 18874376 | tf_op jit(solution)/shard_map/while/body/eval_jaxpr/ppermute | solution.py:16
  1964.6 136.0 %collective-permute-start = (bf16[32,128,768]{2,1,0:T(8,128)(2,1)}, bf16[32,128,768]{2,1,0:T(8,128)(2,1)}, u32[]{:S(2)}, u32[]{:S(2)}) collective-permute-start(bf16[32,128,768]{2,1,0:T(8,128)(2,1)} %get-tuple-element.58), channel_id=1, source_target_pairs={{14,0},{15,1},{0,2},{1,3},{2,4},{3,5},{4,6},{5,7},{6,8},{7,9},{8,1... | collective-permute-start | bytes 18874376 | tf_op jit(solution)/shard_map/while/body/eval_jaxpr/ppermute | solution.py:16
where the time goes:
time: 2140 us; the launch traced here: 2130 us
  waiting for transfers between devices  1360 us (64%)
  matrix products  365 us (17%)
  local copies, waits for them, and re-layouts  182 us (9%)
  other arithmetic  120 us (6%)
  starting transfers between devices  102 us (5%)
    ppermute x7, waiting for transfers between devices, from_behind(): return lax.ppermute(block, axis, route)  983 us
    dot_general x1, matrix products, on_device(): jnp.dot(normed2, fc1_weight, preferred_element_type=jnp.float32) + fc1_bias  126 us
    dot_general x12, matrix products, contract(): return jnp.einsum(form, left, right, precision=FULL_PRECISION)  120 us
    all_to_all x1, waiting for transfers between devices, on_device(): lax.all_to_all(imag_part, 'spatial', split_axis=1, concat_axis=0, tiled=T...  95.7 us
    all_to_all x1, waiting for transfers between devices, on_device(): lax.all_to_all(imag_part, 'spatial', split_axis=0, concat_axis=1, tiled=T...  95.6 us
    all_to_all x1, waiting for transfers between devices, on_device(): lax.all_to_all(real_part, 'spatial', split_axis=1, concat_axis=0, tiled=T...  94.8 us
    dot_general x8, matrix products, block_product(): jnp.einsum('...bi,bio->...bo', values, weight, precision=FULL_PRECISION)  92.7 us
    add x7, other arithmetic, advance(): return (moving, summed + moving.astype(jnp.float32))  92.6 us
  transfers between devices with their start and end apart: 11, of which 11 were waited for; matrix products, arithmetic and copies ran while one was open for 3% of the time, Pallas kernels for 0%

commit v1 on v0

--- a/solution.py
+++ b/solution.py
@@ -139,7 +139,12 @@
     real_part, imag_part = longitude_forward(normed, lon_len)
     real_part, imag_part = (
         lax.all_to_all(real_part, "spatial", split_axis=1, concat_axis=0, tiled=True),
-        lax.all_to_all(imag_part, "spatial", split_axis=1, concat_axis=0, tiled=True),
+        jnp.concatenate(
+            lax.all_to_all(
+                jnp.stack(jnp.split(imag_part, lax.axis_size("spatial"), axis=1)), "spatial", 0, 0
+            ),
+            axis=0,
+        ),
     )
     real_part, imag_part = latitude_work(
         real_part, imag_part, spectral_w1, spectral_b1, spectral_w2, spectral_b2

time: 2140 us -> 2150 us (level)
  no operation moved by 1% of the time
where the time goes in v1:
time: 2150 us; the launch traced here: 2140 us
  waiting for transfers between devices  1360 us (63%)
  matrix products  371 us (17%)
  local copies, waits for them, and re-layouts  185 us (9%)
  other arithmetic  120 us (6%)
  starting transfers between devices  102 us (5%)
    ppermute x7, waiting for transfers between devices, from_behind(): return lax.ppermute(block, axis, route)  983 us
    dot_general x1, matrix products, on_device(): jnp.dot(normed2, fc1_weight, preferred_element_type=jnp.float32) + fc1_bias  126 us
    dot_general x12, matrix products, contract(): return jnp.einsum(form, left, right, precision=FULL_PRECISION)  126 us
    all_to_all x1, waiting for transfers between devices, on_device(): lax.all_to_all(jnp.stack(jnp.split(imag_part, lax.axis_size('spatial'), a...  95.7 us
    all_to_all x1, waiting for transfers between devices, on_device(): lax.all_to_all(imag_part, 'spatial', split_axis=0, concat_axis=1, tiled=T...  95.6 us
    all_to_all x1, waiting for transfers between devices, on_device(): lax.all_to_all(real_part, 'spatial', split_axis=1, concat_axis=0, tiled=T...  93.3 us
    dot_general x8, matrix products, block_product(): jnp.einsum('...bi,bio->...bo', values, weight, precision=FULL_PRECISION)  92.7 us
    add x7, other arithmetic, advance(): return (moving, summed + moving.astype(jnp.float32))  92.6 us
  transfers between devices with their start and end apart: 11, of which 11 were waited for; matrix products, arithmetic and copies ran while one was open for 3% of the time, Pallas kernels for 0%

profile of v1, /device:TPU:0, one launch (start us, length us, event | category | flops | bytes accessed | tf_op | source)
XLA Modules:
  0.0 2139.3 jit_solution(15869377531767128096)
XLA Ops:
  7.6 10.5 negate_bitcast_fusion
  31.2 7.7 all-to-all-start.1
  39.0 12.0 fusion.94
  51.0 6.3 copy.55
  57.3 95.7 %all-to-all-done.1 = f32[16,32,4,768]{3,2,1,0:T(4,128)} async-done(((f32[16,32,4,768]{3,2,1,0:T(4,128)}), f32[16,32,4,768]{3,2,1,0:T(4,128)}, u32[]{:S(2)}, u32[]{:S(2)}) %all-to-all-start.1) | async-done | bytes 6291488 | tf_op jit(solution)/shard_map/all_to_all | solution.py:143
  153.0 28.5 %all-to-all-start = ((f32[32,64,768]{2,0,1:T(8,128)}), f32[32,64,768]{2,0,1:T(8,128)}, u32[]{:S(2)}, u32[]{:S(2)}) async-start(f32[32,64,768]{2,0,1:T(8,128)} %copy.55), calls=%async_computation | async-start | bytes 12582912 | tf_op jit(solution)/shard_map/all_to_all | solution.py:141
  181.6 10.3 fusion.74
  191.8 10.4 fusion.76
  202.2 93.3 %all-to-all-done = f32[32,64,768]{2,0,1:T(8,128)} async-done(((f32[32,64,768]{2,0,1:T(8,128)}), f32[32,64,768]{2,0,1:T(8,128)}, u32[]{:S(2)}, u32[]{:S(2)}) %all-to-all-start) | async-done | bytes 6291488 | tf_op jit(solution)/shard_map/all_to_all | solution.py:141
  302.0 7.9 subtract_bitcast_fusion.1
  309.8 9.9 reshape.97
  319.8 13.7 fusion.58
  333.5 9.9 fusion.60
  343.4 8.2 add_bitcast_fusion.1
  351.6 9.9 reshape.96
  361.4 13.1 add_maximum_fusion
  374.6 9.5 fusion.50
  384.1 9.8 fusion.52
  394.0 9.6 add_maximum_fusion.1
  403.6 14.9 select_bitcast_fusion
  418.5 11.0 copy.66
  429.5 9.6 reshape.99
  439.1 12.2 select_bitcast_fusion.1
  451.4 11.0 copy.65
  462.3 9.6 reshape.98
  471.9 8.3 fusion.144
  480.2 8.7 subtract_bitcast_fusion
  489.4 6.6 copy.68
  496.1 28.2 %all-to-all-start.2 = ((f32[512,4,768]{2,1,0:T(4,128)}), f32[512,4,768]{2,1,0:T(4,128)}, u32[]{:S(2)}, u32[]{:S(2)}) async-start(f32[512,4,768]{2,1,0:T(4,128)} %copy.68), calls=%async_computation.2 | async-start | bytes 12582912 | tf_op jit(solution)/shard_map/all_to_all | solution.py:153
  524.3 8.6 fusion.142
  533.0 6.7 add_bitcast_fusion
  540.1 6.7 copy.72
  546.8 91.5 %all-to-all-done.2 = f32[512,4,768]{2,1,0:T(4,128)} async-done(((f32[512,4,768]{2,1,0:T(4,128)}), f32[512,4,768]{2,1,0:T(4,128)}, u32[]{:S(2)}, u32[]{:S(2)}) %all-to-all-start.2) | async-done | bytes 6291488 | tf_op jit(solution)/shard_map/all_to_all | solution.py:153
  638.4 28.5 %all-to-all-start.3 = ((f32[512,4,768]{2,1,0:T(4,128)}), f32[512,4,768]{2,1,0:T(4,128)}, u32[]{:S(2)}, u32[]{:S(2)}) async-start(f32[512,4,768]{2,1,0:T(4,128)} %copy.72), calls=%async_computation.3 | async-start | bytes 12582912 | tf_op jit(solution)/shard_map/all_to_all | solution.py:154
  670.9 6.7 copy.70
  677.7 7.7 all_to_all.47
  685.4 95.6 %all-to-all-done.3 = f32[512,4,768]{2,1,0:T(4,128)} async-done(((f32[512,4,768]{2,1,0:T(4,128)}), f32[512,4,768]{2,1,0:T(4,128)}, u32[]{:S(2)}, u32[]{:S(2)}) %all-to-all-start.3) | async-done | bytes 6291488 | tf_op jit(solution)/shard_map/all_to_all | solution.py:154
  785.0 6.7 copy.74
  791.7 7.9 all_to_all.51
  799.6 15.1 fusion.150
  814.8 19.1 fusion.278
  838.5 126.4 %fusion.2.clone.6 = bf16[4096,3072]{1,0:T(8,128)(2,1)} fusion(bf16[4096,768]{1,0:T(8,128)(2,1)S(1)} %fusion.47, bf16[768,3072]{1,0:T(8,128)(2,1)} %param.24, f32[3072]{0:T(1024)S(1)} %copy-done.22), kind=kOutput, calls=%fused_computation.4.clone.clone.clone.clone.clone.1 | convolution fusion | flops 20157825024 | bytes 36188160 | tf_op jit(solution)/shard_map/dot_general | solution.py:160
  964.9 26.3 %fusion.49 = bf16[4096,768]{1,0:T(8,128)(2,1)S(1)} fusion(f32[32,128,768]{2,1,0:T(8,128)} %copy-done, bf16[3072,768]{1,0:T(8,128)(2,1)} %param.26, f32[768]{0:T(1024)S(1)} %copy-done.23, bf16[4096,3072]{1,0:T(8,128)(2,1)} %fusion.2.clone.6), kind=kOutput, calls=%fused_computation.62 | convolution fusion | flops 19336790016 | bytes 48761856 | tf_op jit(solution)/shard_map/dot_general | solution.py:163
  1000.0 1127.6 %while.12 = (s32[]{:T(128)}, bf16[32,128,768]{2,1,0:T(8,128)(2,1)}, f32[32,128,768]{2,1,0:T(8,128)}, s32[]{:T(128)}) while((s32[]{:T(128)}, bf16[32,128,768]{2,1,0:T(8,128)(2,1)}, f32[32,128,768]{2,1,0:T(8,128)}, s32[]{:T(128)}) %tuple.26), condition=%wide.region_5.6_spmd, body=%wide.region_4.5_spmd.sunk | while | flops 6291458 | bytes 69206104 | solution.py:174
  1000.3 9.1 collective-permute-start
  1009.3 154.1 %collective-permute-done = bf16[32,128,768]{2,1,0:T(8,128)(2,1)} collective-permute-done((bf16[32,128,768]{2,1,0:T(8,128)(2,1)}, bf16[32,128,768]{2,1,0:T(8,128)(2,1)}, u32[]{:S(2)}, u32[]{:S(2)}) %collective-permute-start) | collective-permute-done | bytes 6291488 | tf_op jit(solution)/shard_map/while/body/eval_jaxpr/ppermute | solution.py:16
  1163.4 6.1 copy.127
  1169.5 13.2 convert_add_fusion.3
  1182.8 140.2 %collective-permute-done = bf16[32,128,768]{2,1,0:T(8,128)(2,1)} collective-permute-done((bf16[32,128,768]{2,1,0:T(8,128)(2,1)}, bf16[32,128,768]{2,1,0:T(8,128)(2,1)}, u32[]{:S(2)}, u32[]{:S(2)}) %collective-permute-start) | collective-permute-done | bytes 6291488 | tf_op jit(solution)/shard_map/while/body/eval_jaxpr/ppermute | solution.py:16
  1323.0 6.1 copy.127
  1329.1 13.2 convert_add_fusion.3
  1342.4 139.4 %collective-permute-done = bf16[32,128,768]{2,1,0:T(8,128)(2,1)} collective-permute-done((bf16[32,128,768]{2,1,0:T(8,128)(2,1)}, bf16[32,128,768]{2,1,0:T(8,128)(2,1)}, u32[]{:S(2)}, u32[]{:S(2)}) %collective-permute-start) | collective-permute-done | bytes 6291488 | tf_op jit(solution)/shard_map/while/body/eval_jaxpr/ppermute | solution.py:16
  1481.8 6.1 copy.127
  1487.9 13.2 convert_add_fusion.3
  1501.1 138.5 %collective-permute-done = bf16[32,128,768]{2,1,0:T(8,128)(2,1)} collective-permute-done((bf16[32,128,768]{2,1,0:T(8,128)(2,1)}, bf16[32,128,768]{2,1,0:T(8,128)(2,1)}, u32[]{:S(2)}, u32[]{:S(2)}) %collective-permute-start) | collective-permute-done | bytes 6291488 | tf_op jit(solution)/shard_map/while/body/eval_jaxpr/ppermute | solution.py:16
  1645.8 13.2 convert_add_fusion.3
  1659.0 137.7 %collective-permute-done = bf16[32,128,768]{2,1,0:T(8,128)(2,1)} collective-permute-done((bf16[32,128,768]{2,1,0:T(8,128)(2,1)}, bf16[32,128,768]{2,1,0:T(8,128)(2,1)}, u32[]{:S(2)}, u32[]{:S(2)}) %collective-permute-start) | collective-permute-done | bytes 6291488 | tf_op jit(solution)/shard_map/while/body/eval_jaxpr/ppermute | solution.py:16
  1796.7 6.1 copy.127
  1802.9 13.2 convert_add_fusion.3
  1816.1 136.8 %collective-permute-done = bf16[32,128,768]{2,1,0:T(8,128)(2,1)} collective-permute-done((bf16[32,128,768]{2,1,0:T(8,128)(2,1)}, bf16[32,128,768]{2,1,0:T(8,128)(2,1)}, u32[]{:S(2)}, u32[]{:S(2)}) %collective-permute-start) | collective-permute-done | bytes 6291488 | tf_op jit(solution)/shard_map/while/body/eval_jaxpr/ppermute | solution.py:16
  1959.1 13.2 convert_add_fusion.3
  1972.3 136.0 %collective-permute-done = bf16[32,128,768]{2,1,0:T(8,128)(2,1)} collective-permute-done((bf16[32,128,768]{2,1,0:T(8,128)(2,1)}, bf16[32,128,768]{2,1,0:T(8,128)(2,1)}, u32[]{:S(2)}, u32[]{:S(2)}) %collective-permute-start) | collective-permute-done | bytes 6291488 | tf_op jit(solution)/shard_map/while/body/eval_jaxpr/ppermute | solution.py:16
  2114.4 13.2 convert_add_fusion.3
  2127.6 11.2 subtract_convert_fusion
  (121 shorter events, 67.3 us)
Async XLA Ops:
  0.6 4.6 copy-start.3
  0.6 7.0 copy-start.16
  0.7 7.0 copy-start.18
  5.2 33.7 %copy-start.10 = (f32[32,128]{1,0:T(8,128)}, f32[32,128]{1,0:T(8,128)S(1)}, u32[]{:S(2)}) copy-start(f32[32,128]{1,0:T(8,128)S(1)} %broadcast_multiply_fusion.1) | copy-start | bytes 49156
  7.6 31.3 %copy-start.12 = (f32[32,128]{1,0:T(8,128)}, f32[32,128]{1,0:T(8,128)S(1)}, u32[]{:S(2)}) copy-start(f32[32,128]{1,0:T(8,128)S(1)} %add_rsqrt_fusion) | copy-start | bytes 49156
  31.2 121.7 %all-to-all-start.1 = ((f32[16,32,4,768]{3,2,1,0:T(4,128)}), f32[16,32,4,768]{3,2,1,0:T(4,128)}, u32[]{:S(2)}, u32[]{:S(2)}) async-start(f32[16,32,4,768]{3,2,1,0:T(4,128)} %fusion.99), calls=%async_computation.1 | async-start | bytes 12582912 | tf_op jit(solution)/shard_map/all_to_all | solution.py:143
  57.3 124.2 %copy-start.14 = (f32[2,8,96]{2,1,0:T(8,128)S(1)}, f32[2,8,96]{2,1,0:T(8,128)}, u32[]{:S(2)}) copy-start(f32[2,8,96]{2,1,0:T(8,128)} %param.19) | copy-start | bytes 18436
  57.3 124.2 %copy-start.15 = (f32[2,8,96]{2,1,0:T(8,128)S(1)}, f32[2,8,96]{2,1,0:T(8,128)}, u32[]{:S(2)}) copy-start(f32[2,8,96]{2,1,0:T(8,128)} %param.21) | copy-start | bytes 18436
  153.0 142.6 %all-to-all-start = ((f32[32,64,768]{2,0,1:T(8,128)}), f32[32,64,768]{2,0,1:T(8,128)}, u32[]{:S(2)}, u32[]{:S(2)}) async-start(f32[32,64,768]{2,0,1:T(8,128)} %copy.55), calls=%async_computation | async-start | bytes 12582912 | tf_op jit(solution)/shard_map/all_to_all | solution.py:141
  202.2 99.7 %slice-start.10 = ((s8[6291456]{0:T(1024)(128)(4,1)}), s8[2097152]{0:T(1024)(128)(4,1)S(1)}, s32[]{:S(2)}) async-start(s8[6291456]{0:T(1024)(128)(4,1)} %bitcast.263), calls=%async_computation.14 | async-start | bytes 4194304
  295.6 6.4 slice-start.11
  299.2 2.7 copy-start.5
  309.8 9.9 copy-start.6
  319.8 13.7 copy-start.1
  319.8 23.6 %slice-start.4 = ((s8[6291456]{0:T(1024)(128)(4,1)}), s8[4194304]{0:T(1024)(128)(4,1)S(1)}, s32[]{:S(2)}) async-start(s8[6291456]{0:T(1024)(128)(4,1)} %bitcast.252), calls=%async_computation.8 | async-start | bytes 8388608
  319.8 23.6 %slice-start.8 = ((s8[6291456]{0:T(1024)(128)(4,1)}), s8[4194304]{0:T(1024)(128)(4,1)S(1)}, s32[]{:S(2)}) async-start(s8[6291456]{0:T(1024)(128)(4,1)} %bitcast.261), calls=%async_computation.12 | async-start | bytes 8388608
  333.5 9.9 slice-start.5
  333.5 9.9 slice-start.9
  361.4 13.2 copy-start.7
  374.6 9.5 copy-start.8
  374.6 19.3 slice-start
  374.6 19.3 slice-start.6
  384.1 9.9 slice-start.1
  384.1 9.9 slice-start.7
  403.6 14.9 copy-start.2
  429.5 9.6 copy-start.9
  496.1 36.9 %slice-start.2 = ((s8[6291456]{0:T(1024)(128)(4,1)}), s8[2097152]{0:T(1024)(128)(4,1)S(1)}, s32[]{:S(2)}) async-start(s8[6291456]{0:T(1024)(128)(4,1)} %bitcast.245), calls=%async_computation.6 | async-start | bytes 4194304
  496.1 142.3 %all-to-all-start.2 = ((f32[512,4,768]{2,1,0:T(4,128)}), f32[512,4,768]{2,1,0:T(4,128)}, u32[]{:S(2)}, u32[]{:S(2)}) async-start(f32[512,4,768]{2,1,0:T(4,128)} %copy.68), calls=%async_computation.2 | async-start | bytes 12582912 | tf_op jit(solution)/shard_map/all_to_all | solution.py:153
  524.3 8.6 slice-start.3
  638.4 142.6 %all-to-all-start.3 = ((f32[512,4,768]{2,1,0:T(4,128)}), f32[512,4,768]{2,1,0:T(4,128)}, u32[]{:S(2)}, u32[]{:S(2)}) async-start(f32[512,4,768]{2,1,0:T(4,128)} %copy.72), calls=%async_computation.3 | async-start | bytes 12582912 | tf_op jit(solution)/shard_map/all_to_all | solution.py:154
  799.6 15.2 copy-start.11
  799.6 15.2 copy-start.13
  799.6 15.2 copy-start.17
  799.6 15.2 copy-start.19
  833.9 4.6 copy-start
  833.9 1.5 copy-start.20
  833.9 1.5 copy-start.21
  835.5 3.1 copy-start.22
  838.5 126.4 %copy-start.23 = (f32[768]{0:T(1024)S(1)}, f32[768]{0:T(1024)}, u32[]{:S(2)}) copy-start(f32[768]{0:T(1024)} %param.27) | copy-start | bytes 9220
  991.1 8.9 copy-start.4
  1000.3 163.1 %collective-permute-start = (bf16[32,128,768]{2,1,0:T(8,128)(2,1)}, bf16[32,128,768]{2,1,0:T(8,128)(2,1)}, u32[]{:S(2)}, u32[]{:S(2)}) collective-permute-start(bf16[32,128,768]{2,1,0:T(8,128)(2,1)} %get-tuple-element.58), channel_id=1, source_target_pairs={{14,0},{15,1},{0,2},{1,3},{2,4},{3,5},{4,6},{5,7},{6,8},{7,9},{8,1... | collective-permute-start | bytes 18874376 | tf_op jit(solution)/shard_map/while/body/eval_jaxpr/ppermute | solution.py:16
  1182.8 140.2 %collective-permute-start = (bf16[32,128,768]{2,1,0:T(8,128)(2,1)}, bf16[32,128,768]{2,1,0:T(8,128)(2,1)}, u32[]{:S(2)}, u32[]{:S(2)}) collective-permute-start(bf16[32,128,768]{2,1,0:T(8,128)(2,1)} %get-tuple-element.58), channel_id=1, source_target_pairs={{14,0},{15,1},{0,2},{1,3},{2,4},{3,5},{4,6},{5,7},{6,8},{7,9},{8,1... | collective-permute-start | bytes 18874376 | tf_op jit(solution)/shard_map/while/body/eval_jaxpr/ppermute | solution.py:16
  1342.4 139.4 %collective-permute-start = (bf16[32,128,768]{2,1,0:T(8,128)(2,1)}, bf16[32,128,768]{2,1,0:T(8,128)(2,1)}, u32[]{:S(2)}, u32[]{:S(2)}) collective-permute-start(bf16[32,128,768]{2,1,0:T(8,128)(2,1)} %get-tuple-element.58), channel_id=1, source_target_pairs={{14,0},{15,1},{0,2},{1,3},{2,4},{3,5},{4,6},{5,7},{6,8},{7,9},{8,1... | collective-permute-start | bytes 18874376 | tf_op jit(solution)/shard_map/while/body/eval_jaxpr/ppermute | solution.py:16
  1501.1 138.5 %collective-permute-start = (bf16[32,128,768]{2,1,0:T(8,128)(2,1)}, bf16[32,128,768]{2,1,0:T(8,128)(2,1)}, u32[]{:S(2)}, u32[]{:S(2)}) collective-permute-start(bf16[32,128,768]{2,1,0:T(8,128)(2,1)} %get-tuple-element.58), channel_id=1, source_target_pairs={{14,0},{15,1},{0,2},{1,3},{2,4},{3,5},{4,6},{5,7},{6,8},{7,9},{8,1... | collective-permute-start | bytes 18874376 | tf_op jit(solution)/shard_map/while/body/eval_jaxpr/ppermute | solution.py:16
  1659.0 137.7 %collective-permute-start = (bf16[32,128,768]{2,1,0:T(8,128)(2,1)}, bf16[32,128,768]{2,1,0:T(8,128)(2,1)}, u32[]{:S(2)}, u32[]{:S(2)}) collective-permute-start(bf16[32,128,768]{2,1,0:T(8,128)(2,1)} %get-tuple-element.58), channel_id=1, source_target_pairs={{14,0},{15,1},{0,2},{1,3},{2,4},{3,5},{4,6},{5,7},{6,8},{7,9},{8,1... | collective-permute-start | bytes 18874376 | tf_op jit(solution)/shard_map/while/body/eval_jaxpr/ppermute | solution.py:16
  1816.1 136.8 %collective-permute-start = (bf16[32,128,768]{2,1,0:T(8,128)(2,1)}, bf16[32,128,768]{2,1,0:T(8,128)(2,1)}, u32[]{:S(2)}, u32[]{:S(2)}) collective-permute-start(bf16[32,128,768]{2,1,0:T(8,128)(2,1)} %get-tuple-element.58), channel_id=1, source_target_pairs={{14,0},{15,1},{0,2},{1,3},{2,4},{3,5},{4,6},{5,7},{6,8},{7,9},{8,1... | collective-permute-start | bytes 18874376 | tf_op jit(solution)/shard_map/while/body/eval_jaxpr/ppermute | solution.py:16
  1972.3 136.0 %collective-permute-start = (bf16[32,128,768]{2,1,0:T(8,128)(2,1)}, bf16[32,128,768]{2,1,0:T(8,128)(2,1)}, u32[]{:S(2)}, u32[]{:S(2)}) collective-permute-start(bf16[32,128,768]{2,1,0:T(8,128)(2,1)} %get-tuple-element.58), channel_id=1, source_target_pairs={{14,0},{15,1},{0,2},{1,3},{2,4},{3,5},{4,6},{5,7},{6,8},{7,9},{8,1... | collective-permute-start | bytes 18874376 | tf_op jit(solution)/shard_map/while/body/eval_jaxpr/ppermute | solution.py:16
